TPU v7x, 128 devices: a whole 4x4x4 slice. The times are simulated.
128 devices in a mesh: dp: 8 (over z_hi, x), shard: 16 (over y, z_lo, core).
Axes of the slice: x: 4, y: 4, z: 4 (z_hi: 2, z_lo: 2; z = z_hi * 2 + z_lo), core: 2. Of those that a mesh axis runs over, the one named last changes fastest.
Arguments:
- gradients: bfloat16 [8, 8, 1572864], P('dp', None, 'shard'), may hold values from -32 to 32
- master: float32 [12582912], P(('dp', 'shard'))
- moment: float32 [12582912], P(('dp', 'shard')), may hold values from -1.5 to 1.5
- second: float32 [12582912], P(('dp', 'shard')), may hold values from 0.05 to 2
- segment_ids: int32 [98304], P(('dp', 'shard')), may hold values from 0 to 63, never falling along the last dimension, each value on 1 to 3072 neighbouring positions
Outputs:
- weights: bfloat16 [8, 1572864], P(None, 'shard')
- new_master: float32 [12582912], P(('dp', 'shard'))
- new_moment: float32 [12582912], P(('dp', 'shard'))
- new_second: float32 [12582912], P(('dp', 'shard'))
Inputs may be any that keep to these rules, and one draw needn't show every extreme that they name: segment_ids never falls along the flat vector; each tensor has 1 to 3072 blocks and one has exactly 3072.
All inputs are finite; a program needn't handle non-finite values.
Results may differ from a plain program's by a relative error of at most 0.0004.
Values may be sent and summed in bfloat16 or wider, within the bound.
A program may use at most 64 MiB of HBM per device.

v0:
```python
import jax
import jax.numpy as jnp
from jax import lax
from jax.sharding import Mesh
from jax.sharding import PartitionSpec as P

DP = ("dp_0", "dp_1")
SHARD = ("shard_0", "shard_1", "shard_2")
DP_SHARD = ("dp_0", "dp_1", "shard_0", "shard_1", "shard_2")


first_fix = 1.0 - 0.9**20
second_fix = 1.0 - 0.999**20
learn_rate = 0.2
decay_rate = 0.01
tiny_eps = 1e-06


def one_axis_at_a_time(array, axes):
    for axis in axes:
        array = lax.psum(array, axis)
    return array


def joined_along(pieces, dim):
    lengths = list(pieces.shape[1:])
    lengths[dim] *= pieces.shape[0]
    return jnp.moveaxis(pieces, 0, dim).reshape(lengths)


def copy_for_each(array, axis):
    copies = jnp.broadcast_to(array, (lax.axis_size(axis), *array.shape))
    return lax.all_to_all(copies, axis, split_axis=0, concat_axis=0, tiled=True)


def gather_directly(array, axis, dim):
    return joined_along(copy_for_each(array, axis), dim)


def moments(summed, master_part, moment_part, second_part, replicas):
    grad = summed / replicas
    next_moment = 0.9 * moment_part + 0.1 * grad
    next_second = 0.999 * second_part + 0.001 * grad * grad
    update_dir = (
        next_moment / first_fix / (jnp.sqrt(next_second / second_fix) + tiny_eps)
        + decay_rate * master_part
    )
    return (next_moment, next_second, update_dir)


def tensor_sums(values, onehot):
    block_sq = jnp.sum((values * values).reshape(onehot.shape[0], -1), axis=1)
    return jnp.dot(block_sq, onehot, precision=lax.Precision.HIGHEST)


def on_device(gradients, master, moment, second, segment_ids):
    replicas = lax.axis_size(DP)
    tensors = lax.axis_size(DP) * lax.axis_size(SHARD) // 2
    blocks = segment_ids.shape[0]
    onehot = (segment_ids[:, None] == jnp.arange(tensors, dtype=jnp.int32)[None, :]).astype(
        jnp.float32
    )
    received = lax.all_to_all(gradients[0], DP, split_axis=0, concat_axis=0, tiled=True)
    summed = jnp.sum(received.astype(jnp.float32), axis=0)
    new_moment, new_second, update_dir = moments(summed, master, moment, second, replicas)
    weight_sq, update_sq = (
        one_axis_at_a_time(tensor_sums(master, onehot), DP_SHARD),
        one_axis_at_a_time(tensor_sums(update_dir, onehot), DP_SHARD),
    )
    trust = jnp.sqrt(weight_sq) / (jnp.sqrt(update_sq) + tiny_eps)
    block_trust = jnp.dot(onehot, trust, precision=lax.Precision.HIGHEST)
    new_master = master - learn_rate * (
        update_dir.reshape(blocks, -1) * block_trust[:, None]
    ).reshape(-1)
    rounded = new_master.astype(jnp.bfloat16)[None, :]
    weights = gather_directly(rounded, DP, 0)
    return (weights, new_master, new_moment, new_second)


def solution(mesh):
    torus = Mesh(
        mesh.devices.reshape(2, 4, 4, 2, 2), ("dp_0", "dp_1", "shard_0", "shard_1", "shard_2")
    )
    return jax.shard_map(
        on_device,
        mesh=torus,
        in_specs=(P(DP, None, SHARD), P(DP_SHARD), P(DP_SHARD), P(DP_SHARD), P(DP_SHARD)),
        out_specs=(P(None, SHARD), P(DP_SHARD), P(DP_SHARD), P(DP_SHARD)),
        check_vma=False,
    )
```

profile of v0, /device:TPU:0, one launch (start us, length us, event | category | flops | bytes accessed | tf_op | source)
XLA Modules:
  0.0 131.7 jit_solution(17424147377295384235)
XLA Ops:
  0.6 0.5 broadcast.10
  1.2 3.2 %reduce.3 = bf16[8,98304]{1,0:T(8,128)(2,1)S(1)} reduce(bf16[8,1,98304]{2,0,1:T(8,128)(2,1)} %bitcast.24, bf16[]{:T(256)} %broadcast.10), dimensions={1}, to_apply=%copy.10.reduce_sub_computation | reduce | bytes 3145730 | tf_op jit(solution)/shard_map/all_to_all | solution.py:63
  4.4 1.4 %reshape.36 = bf16[8,2,49152]{2,1,0:T(2,128)(2,1)S(1)} reshape(bf16[8,98304]{1,0:T(8,128)(2,1)S(1)} %reduce.3) | data formatting | bytes 3145728
  5.8 30.4 %all_to_all.14 = bf16[8,2,49152]{2,1,0:T(2,128)(2,1)} all-to-all(bf16[8,2,49152]{2,1,0:T(2,128)(2,1)S(1)} %reshape.36), channel_id=1, replica_groups=mesh['dp_0'=2,'dp_1'=4,'shard_0'=4,'shard_1'=2,'shard_2'=2] {'dp_0','dp_1'}, dimensions={0} | all-to-all | bytes 3145728 | tf_op jit(solution)/shard_map/all_to_all | solution.py:63
  36.2 4.7 %reshape.37 = bf16[8,1,98304]{2,1,0:T(2,128)(2,1)S(1)} reshape(bf16[8,2,49152]{2,1,0:T(2,128)(2,1)} %all_to_all.14) | data formatting | bytes 3145728
  40.9 0.0 copy-start
  40.9 0.0 copy-start.3
  40.9 0.0 copy-start.4
  40.9 4.1 %convert_reduce_fusion = f32[98304]{0:T(1024)S(1)} fusion(bf16[8,1,98304]{2,1,0:T(2,128)(2,1)S(1)} %reshape.37), kind=kLoop, calls=%fused_computation | loop fusion | flops 1474560 | bytes 1966080 | tf_op jit(solution)/shard_map/reduce_sum | solution.py:64
  45.1 0.0 copy-done
  45.1 0.0 copy-done.3
  45.1 0.0 copy-done.4
  45.1 0.0 copy-start.5
  45.1 0.4 bitcast_reduce_fusion.1
  45.6 0.0 copy-start.1
  45.6 0.0 copy-start.2
  45.6 0.2 copy-done.5
  45.8 0.3 convolution_bitcast_fusion.1
  46.1 0.3 convolution_bitcast_fusion
  46.5 6.4 %all-reduce.4 = (f32[64]{0:T(128)S(1)}, f32[64]{0:T(128)S(1)}) all-reduce(f32[64]{0:T(128)S(1)} %convolution_bitcast_fusion, f32[64]{0:T(128)S(1)} %convolution_bitcast_fusion.1), channel_id=1, replica_groups=mesh['dp_0'=2,'dp_1'=4,'shard_0'=4,'shard_1'=2,'shard_2'=2] {'dp_0'}, use_global_device_ids=true, to_apply=%region_8.0 | all-reduce | flops 128 | bytes 1024 | tf_op jit(solution)/shard_map/psum | solution.py:21
  52.9 9.0 %all-reduce.1 = (f32[64]{0:T(128)S(1)}, f32[64]{0:T(128)S(1)}) all-reduce(f32[64]{0:T(128)S(1)} %get-tuple-element.14, f32[64]{0:T(128)S(1)} %get-tuple-element.15), channel_id=1, replica_groups=mesh['dp_0'=2,'dp_1'=4,'shard_0'=4,'shard_1'=2,'shard_2'=2] {'dp_1'}, use_global_device_ids=true, to_apply=%region_9.0 | all-reduce | flops 128 | bytes 1024 | tf_op jit(solution)/shard_map/psum | solution.py:21
  61.9 10.7 %all-reduce = (f32[64]{0:T(128)S(1)}, f32[64]{0:T(128)S(1)}) all-reduce(f32[64]{0:T(128)S(1)} %get-tuple-element.8, f32[64]{0:T(128)S(1)} %get-tuple-element.9), channel_id=1, replica_groups=mesh['dp_0'=2,'dp_1'=4,'shard_0'=4,'shard_1'=2,'shard_2'=2] {'shard_0'}, use_global_device_ids=true, to_apply=%region_10.0 | all-reduce | flops 128 | bytes 1024 | tf_op jit(solution)/shard_map/psum | solution.py:21
  72.6 4.9 %all-reduce.3 = (f32[64]{0:T(128)S(1)}, f32[64]{0:T(128)S(1)}) all-reduce(f32[64]{0:T(128)S(1)} %get-tuple-element.6, f32[64]{0:T(128)S(1)} %get-tuple-element.7), channel_id=1, replica_groups=mesh['dp_0'=2,'dp_1'=4,'shard_0'=4,'shard_1'=2,'shard_2'=2] {'shard_1'}, use_global_device_ids=true, to_apply=%region_11.0 | all-reduce | flops 128 | bytes 1024 | tf_op jit(solution)/shard_map/psum | solution.py:21
  77.5 2.6 %all-reduce.2 = (f32[64]{0:T(128)S(1)}, f32[64]{0:T(128)S(1)}) all-reduce(f32[64]{0:T(128)S(1)} %get-tuple-element.12, f32[64]{0:T(128)S(1)} %get-tuple-element.13), channel_id=1, replica_groups=mesh['dp_0'=2,'dp_1'=4,'shard_0'=4,'shard_1'=2,'shard_2'=2] {'shard_2'}, use_global_device_ids=true, to_apply=%region_12.0 | all-reduce | flops 128 | bytes 1024 | tf_op jit(solution)/shard_map/psum | solution.py:21
  80.2 0.4 convolution_reduce_fusion
  80.6 1.0 fusion.10
  81.6 0.0 copy-done.1
  81.6 0.0 copy-done.2
  81.6 1.6 %broadcast_in_dim.2 = bf16[8,1,98304]{2,1,0:T(2,128)(2,1)S(1)} broadcast(bf16[98304]{0:T(1024)(128)(2,1)S(1)} %get-tuple-element.16), dimensions={2} | broadcast | bytes 1769472 | tf_op jit(solution)/shard_map/broadcast_in_dim | solution.py:32
  83.2 11.6 %reduce.4 = bf16[8,98304]{1,0:T(8,128)(2,1)} reduce(bf16[8,1,98304]{2,1,0:T(2,128)(2,1)S(1)} %broadcast_in_dim.2, bf16[]{:T(256)} %broadcast.10), dimensions={1}, to_apply=%broadcast_in_dim.2.reduce_sub_computation | reduce | bytes 3145730 | tf_op jit(solution)/shard_map/broadcast_in_dim | solution.py:32
  94.8 2.8 %reshape.38 = bf16[8,2,49152]{2,1,0:T(2,128)(2,1)S(1)} reshape(bf16[8,98304]{1,0:T(8,128)(2,1)} %reduce.4) | data formatting | bytes 3145728
  97.5 26.6 %all_to_all.15 = bf16[8,2,49152]{2,1,0:T(2,128)(2,1)} all-to-all(bf16[8,2,49152]{2,1,0:T(2,128)(2,1)S(1)} %reshape.38), channel_id=1, replica_groups=mesh['dp_0'=2,'dp_1'=4,'shard_0'=4,'shard_1'=2,'shard_2'=2] {'dp_0','dp_1'}, dimensions={0} | all-to-all | bytes 3145728 | tf_op jit(solution)/shard_map/all_to_all | solution.py:33
  124.1 4.7 %reshape.39 = bf16[8,1,98304]{2,1,0:T(2,128)(2,1)S(1)} reshape(bf16[8,2,49152]{2,1,0:T(2,128)(2,1)} %all_to_all.15) | data formatting | bytes 3145728
  128.8 2.9 %copy.13 = bf16[8,1,98304]{2,0,1:T(8,128)(2,1)} copy(bf16[8,1,98304]{2,1,0:T(2,128)(2,1)S(1)} %reshape.39) | data formatting | bytes 3145728
  (2 shorter events, 0.0 us)
Async XLA Ops:
  40.9 4.2 %copy-start = (f32[98304]{0:T(1024)S(1)}, f32[98304]{0:T(1024)}, u32[]{:S(2)}) copy-start(f32[98304]{0:T(1024)} %param.6) | copy-start | bytes 1179652
  40.9 4.2 %copy-start.3 = (f32[98304]{0:T(1024)S(1)}, f32[98304]{0:T(1024)}, u32[]{:S(2)}) copy-start(f32[98304]{0:T(1024)} %param.7) | copy-start | bytes 1179652
  40.9 4.2 %copy-start.4 = (f32[98304]{0:T(1024)S(1)}, f32[98304]{0:T(1024)}, u32[]{:S(2)}) copy-start(f32[98304]{0:T(1024)} %param.8) | copy-start | bytes 1179652
  45.1 0.7 copy-start.5
  45.6 36.0 %copy-start.1 = (f32[98304]{0:T(1024)}, f32[98304]{0:T(1024)S(1)}, u32[]{:S(2)}) copy-start(f32[98304]{0:T(1024)S(1)} %get-tuple-element.18) | copy-start | bytes 1179652
  45.6 36.0 %copy-start.2 = (f32[98304]{0:T(1024)}, f32[98304]{0:T(1024)S(1)}, u32[]{:S(2)}) copy-start(f32[98304]{0:T(1024)S(1)} %get-tuple-element.19) | copy-start | bytes 1179652
where the time goes:
time: 133 us; the launch traced here: 132 us
  blocking collectives  90.7 us (68%)
  other arithmetic  20.4 us (15%)
  local copies, waits for them, and re-layouts  18.7 us (14%)
    psum x5, blocking collectives, one_axis_at_a_time(): array = lax.psum(array, axis)  33.7 us
    all_to_all x1, blocking collectives, on_device(): lax.all_to_all(gradients[0], DP, split_axis=0, concat_axis=0, tiled=True)  30.4 us
    all_to_all x1, blocking collectives, copy_for_each(): return lax.all_to_all(copies, axis, split_axis=0, concat_axis=0, tiled=True)  26.6 us
    unnamed x17, local copies, waits for them, and re-layouts  16.6 us
    broadcast_in_dim x1, other arithmetic, copy_for_each(): copies = jnp.broadcast_to(array, (lax.axis_size(axis), *array.shape))  11.6 us
    reduce_sum x1, other arithmetic, on_device(): summed = jnp.sum(received.astype(jnp.float32), axis=0)  4.14 us
    all_to_all x1, other arithmetic, on_device(): lax.all_to_all(gradients[0], DP, split_axis=0, concat_axis=0, tiled=True)  3.23 us

commit v1 on v0

v1 whole, which is shorter than its diff:
```python
import functools

import jax
import jax.numpy as jnp
from jax import lax
from jax.experimental import pallas as pl
from jax.experimental.pallas import tpu as pltpu
from jax.sharding import Mesh
from jax.sharding import PartitionSpec as P

AXES = ("zh", "x", "y", "zl", "core")
DP = ("zh", "x")
SHARD = ("y", "zl", "core")
DP_SHARD = AXES
MESH = pl.DeviceIdType.MESH

first_fix = 1.0 - 0.9**20
second_fix = 1.0 - 0.999**20
learn_rate = 0.2
decay_rate = 0.01
tiny_eps = 1e-06

REPLICAS = 8
TENSORS = 64
BLOCKS = 768
LANES = 128
CHUNK = 128
CHUNKS = BLOCKS // CHUNK
SUB = 32
PIECE = 64
PIECES = BLOCKS // PIECE
REACH = 4
LAG = 4
HIGH = lax.Precision.HIGHEST

STEPS = ((1, 0), (3, 0), (0, 1), (2, 1), (2, 0), (1, 1), (3, 1))
X_STEPS = (1, 3, 2)
OFFSETS = tuple(range(-REACH, 0)) + tuple(range(1, REACH + 1))


def place():
    return {axis: lax.axis_index(axis) for axis in AXES}


def replica_at(here, x_step, z_step):
    there = dict(here)
    there["x"] = lax.rem(here["x"] + x_step, 4)
    there["zh"] = lax.rem(here["zh"] + z_step, 2)
    return there


def row_of(there):
    return there["zh"] * 4 + there["x"]


def flat_neighbour(here, offset):
    rank = (((here["zh"] * 4 + here["x"]) * 4 + here["y"]) * 2 + here["zl"]) * 2 + here["core"]
    rank = lax.rem(rank + offset + 128, 128)
    return {
        "zh": rank // 64,
        "x": lax.rem(rank // 16, 4),
        "y": lax.rem(rank // 4, 4),
        "zl": lax.rem(rank // 2, 2),
        "core": lax.rem(rank, 2),
    }


def remote(src, dst, send_sem, recv_sem, there):
    return pltpu.make_async_remote_copy(
        src_ref=src,
        dst_ref=dst,
        send_sem=send_sem,
        recv_sem=recv_sem,
        device_id=there,
        device_id_type=MESH,
    )


def kernel(
    grad_hbm, master_hbm, moment_hbm, second_hbm, ids_hbm,
    weights_out, master_out, moment_out, second_out,
    grad_in, rows, got, master, moment, second, update, ids, squares, sums,
    mine, theirs, spread, gathered, packed,
    load_sem, state_sem, send_sem, recv_sem, sum_send, sum_recv,
    out_send, out_recv, store_sem, state_out_sem,
):
    here = place()
    me = row_of(here)
    peers = [replica_at(here, a, b) for a, b in STEPS]
    neighbours = [flat_neighbour(here, k) for k in OFFSETS]

    def load(c):
        cols = pl.ds(pl.multiple_of(c * CHUNK * LANES, CHUNK * LANES), CHUNK * LANES)
        return pltpu.make_async_copy(grad_hbm.at[:, cols], grad_in.at[:, cols], load_sem.at[c])

    for c in range(CHUNKS):
        load(c).start()
    state_loads = [
        pltpu.make_async_copy(src, dst, state_sem.at[i])
        for i, (src, dst) in enumerate(
            ((ids_hbm, ids), (master_hbm, master), (moment_hbm, moment), (second_hbm, second))
        )
    ]
    for copy in state_loads:
        copy.start()

    barrier = pltpu.get_barrier_semaphore()
    for there in peers + neighbours:
        pl.semaphore_signal(barrier, inc=1, device_id=there, device_id_type=MESH)

    def split_rows(c):
        load(c).wait()

        def tile(t, carry):
            at = c * CHUNK + t * 8
            for i in range(8):
                cols = pl.ds(pl.multiple_of((at + i) * LANES, LANES), LANES)
                spread[pl.ds(pl.multiple_of((t * 8 + i) * 8, 8), 8), :] = grad_in[:, cols].astype(
                    jnp.float32
                )
            return carry

        lax.fori_loop(0, CHUNK // 8, tile, 0)
        for r in range(REPLICAS):
            for h in range(CHUNK // SUB):
                piece = spread[pl.ds(h * SUB * 8 + r, SUB, stride=8), :]
                rows[r, pl.ds(pl.multiple_of(c * CHUNK + h * SUB, SUB), SUB), :] = piece.astype(
                    jnp.bfloat16
                )

    def exchange(c, k):
        part = pl.ds(pl.multiple_of(c * CHUNK, CHUNK), CHUNK)
        return remote(
            rows.at[row_of(peers[k]), part], got.at[k, part],
            send_sem.at[c, k], recv_sem.at[c, k], peers[k],
        )

    def send_chunk(c, carry):
        split_rows(c)

        @pl.when(c == 0)
        def _():
            pl.semaphore_wait(barrier, len(peers) + len(neighbours))

        for k in range(len(STEPS)):
            exchange(c, k).start()
        return carry

    lax.fori_loop(0, CHUNKS, send_chunk, 0)

    for copy in state_loads:
        copy.wait()

    def onehot(c):
        tensor = lax.broadcasted_iota(jnp.int32, (TENSORS, CHUNK), 0)
        return (tensor == ids[pl.ds(c, 1), :]).astype(jnp.float32)

    sums[...] = jnp.zeros_like(sums)

    def weigh(c, carry):
        values = master[pl.ds(pl.multiple_of(c * CHUNK, CHUNK), CHUNK), :]
        sums[:TENSORS, :] += jnp.dot(
            onehot(c), values * values, precision=HIGH, preferred_element_type=jnp.float32
        )
        return carry

    lax.fori_loop(0, CHUNKS, weigh, 0)

    def step_chunk(c, carry):
        for k in range(len(STEPS)):
            exchange(c, k).wait_recv()
        for h in range(CHUNK // SUB):
            part = pl.ds(pl.multiple_of(c * CHUNK + h * SUB, SUB), SUB)
            total = rows[me, part, :].astype(jnp.float32)
            for k in range(len(STEPS)):
                total = total + got[k, part, :].astype(jnp.float32)
            grad = total / REPLICAS
            next_moment = 0.9 * moment[part, :] + 0.1 * grad
            next_second = 0.999 * second[part, :] + 0.001 * grad * grad
            change = (
                next_moment / first_fix / (jnp.sqrt(next_second / second_fix) + tiny_eps)
                + decay_rate * master[part, :]
            )
            moment[part, :] = next_moment
            second[part, :] = next_second
            update[part, :] = change
            squares[pl.ds(h * SUB, SUB), :] = change * change
        sums[TENSORS:, :] += jnp.dot(
            onehot(c), squares[...], precision=HIGH, preferred_element_type=jnp.float32
        )
        return carry

    lax.fori_loop(0, CHUNKS, step_chunk, 0)

    ones = jnp.ones((8, LANES), jnp.float32)
    mine[...] = lax.dot_general(
        ones, sums[...], (((1,), (1,)), ((), ())), precision=HIGH,
        preferred_element_type=jnp.float32,
    )
    swaps = [
        remote(mine, theirs.at[i], sum_send.at[i], sum_recv.at[i], neighbours[len(OFFSETS) - 1 - i])
        for i in range(len(OFFSETS))
    ]
    for copy in swaps:
        copy.start()
    state_stores = [
        pltpu.make_async_copy(moment, moment_out, state_out_sem.at[0]),
        pltpu.make_async_copy(second, second_out, state_out_sem.at[1]),
    ]
    for copy in state_stores:
        copy.start()
    for copy in swaps:
        copy.wait_recv()
    total = mine[...]
    for i in range(len(OFFSETS)):
        total = total + theirs[i]
    trust = jnp.sqrt(total) / (jnp.sqrt(pltpu.roll(total, TENSORS, 1)) + tiny_eps)
    trust_row = trust[:1, :]
    diagonal = lax.broadcasted_iota(jnp.int32, (TENSORS, LANES), 0) == lax.broadcasted_iota(
        jnp.int32, (TENSORS, LANES), 1
    )
    trust_of = jnp.sum(jnp.where(diagonal, trust_row, 0.0), axis=1, keepdims=True)
    trust_of = jnp.broadcast_to(trust_of, (TENSORS, LANES))

    partner = replica_at(here, 0, 1)
    beside = [replica_at(here, a, 0) for a in X_STEPS]
    behind = [replica_at(here, 4 - a, 0) for a in X_STEPS]
    direct_to = [partner] + beside
    direct_from = [partner] + behind
    far_from = [replica_at(here, 4 - a, 1) for a in X_STEPS]

    def piece_of(p):
        return pl.ds(pl.multiple_of(p * PIECE, PIECE), PIECE)

    def direct(p, i):
        block = gathered.at[me, piece_of(p)]
        return remote(block, block, out_send.at[p, i], out_recv.at[p, i], direct_to[i])

    def arrived(p, i, source):
        block = gathered.at[row_of(source), piece_of(p)]
        return remote(block, block, out_send.at[p, i], out_recv.at[p, i], partner)

    def onward_x(p, j):
        block = gathered.at[row_of(partner), piece_of(p)]
        return remote(block, block, out_send.at[p, 4 + j], out_recv.at[p, 4 + j], beside[j])

    def onward_z(p, j):
        block = gathered.at[row_of(behind[j]), piece_of(p)]
        return remote(block, block, out_send.at[p, 4 + j], out_recv.at[p, 4 + j], partner)

    def finish_chunk(c, carry):
        trust_block = lax.dot_general(
            onehot(c), trust_of, (((0,), (0,)), ((), ())), precision=HIGH,
            preferred_element_type=jnp.float32,
        )
        part = pl.ds(pl.multiple_of(c * CHUNK, CHUNK), CHUNK)
        new_master = master[part, :] - learn_rate * (update[part, :] * trust_block)
        master[part, :] = new_master
        gathered[me, part, :] = new_master.astype(jnp.bfloat16)
        for half in range(CHUNK // PIECE):
            for i in range(4):
                direct(c * (CHUNK // PIECE) + half, i).start()
        return carry

    lax.fori_loop(0, CHUNKS, finish_chunk, 0)
    state_stores.append(pltpu.make_async_copy(master, master_out, state_out_sem.at[2]))
    state_stores[2].start()

    def z_first(p):
        return lax.rem(p * 5, 12) < 5

    def forward(p):
        @pl.when(z_first(p))
        def _():
            arrived(p, 0, partner).wait_recv()
            for j in range(3):
                onward_x(p, j).start()

        @pl.when(jnp.logical_not(z_first(p)))
        def _():
            for j in range(3):
                arrived(p, 1 + j, behind[j]).wait_recv()
                onward_z(p, j).start()

    def store(p):
        cols = pl.ds(pl.multiple_of(p * PIECE * LANES, PIECE * LANES), PIECE * LANES)
        return pltpu.make_async_copy(packed.at[:, cols], weights_out.at[:, cols], store_sem.at[p])

    def collect(p):
        @pl.when(z_first(p))
        def _():
            for j in range(3):
                arrived(p, 1 + j, behind[j]).wait_recv()

        @pl.when(jnp.logical_not(z_first(p)))
        def _():
            arrived(p, 0, partner).wait_recv()

        for j in range(3):
            arrived(p, 4 + j, far_from[j]).wait_recv()
        for r in range(REPLICAS):
            spread[pl.ds(r, PIECE, stride=8), :] = gathered[r, piece_of(p), :].astype(jnp.float32)

        def tile(t, carry):
            for i in range(8):
                at = t * 8 + i
                cols = pl.ds(pl.multiple_of((p * PIECE + at) * LANES, LANES), LANES)
                packed[:, cols] = spread[pl.ds(pl.multiple_of(at * 8, 8), 8), :].astype(
                    jnp.bfloat16
                )
            return carry

        lax.fori_loop(0, PIECE // 8, tile, 0)
        store(p).start()

    def gather_step(s, carry):
        @pl.when(s < PIECES)
        def _():
            forward(s)

        @pl.when(s >= LAG)
        def _():
            collect(s - LAG)

        return carry

    lax.fori_loop(0, PIECES + LAG, gather_step, 0)

    def drain(c, carry):
        for k in range(len(STEPS)):
            exchange(c, k).wait_send()
        return carry

    lax.fori_loop(0, CHUNKS, drain, 0)

    def drain_out(p, carry):
        for i in range(7):
            remote(
                gathered.at[me, piece_of(p)], gathered.at[me, piece_of(p)],
                out_send.at[p, i], out_recv.at[p, i], partner,
            ).wait_send()
        store(p).wait()
        return carry

    lax.fori_loop(0, PIECES, drain_out, 0)
    for copy in swaps:
        copy.wait_send()
    for copy in state_stores:
        copy.wait()


def on_device(gradients, master, moment, second, segment_ids):
    flat = master.shape[0]
    tall = (BLOCKS, LANES)
    f32, bf16 = jnp.float32, jnp.bfloat16
    any_spec = pl.BlockSpec(memory_space=pl.ANY)
    dma = pltpu.SemaphoreType.DMA
    weights, new_master, new_moment, new_second = pl.pallas_call(
        kernel,
        out_shape=(
            jax.ShapeDtypeStruct((REPLICAS, flat), bf16),
            jax.ShapeDtypeStruct(tall, f32),
            jax.ShapeDtypeStruct(tall, f32),
            jax.ShapeDtypeStruct(tall, f32),
        ),
        in_specs=[pl.BlockSpec(memory_space=pltpu.HBM)] * 5,
        out_specs=(any_spec,) * 4,
        scratch_shapes=[
            pltpu.VMEM((REPLICAS, flat), bf16),
            pltpu.VMEM((REPLICAS, BLOCKS, LANES), bf16),
            pltpu.VMEM((len(STEPS), BLOCKS, LANES), bf16),
            pltpu.VMEM(tall, f32),
            pltpu.VMEM(tall, f32),
            pltpu.VMEM(tall, f32),
            pltpu.VMEM(tall, f32),
            pltpu.VMEM((CHUNKS, CHUNK), jnp.int32),
            pltpu.VMEM((CHUNK, LANES), f32),
            pltpu.VMEM((2 * TENSORS, LANES), f32),
            pltpu.VMEM((8, LANES), f32),
            pltpu.VMEM((len(OFFSETS), 8, LANES), f32),
            pltpu.VMEM((CHUNK * 8, LANES), f32),
            pltpu.VMEM((REPLICAS, BLOCKS, LANES), bf16),
            pltpu.VMEM((REPLICAS, flat), bf16),
            dma((CHUNKS,)),
            dma((4,)),
            dma((CHUNKS, len(STEPS))),
            dma((CHUNKS, len(STEPS))),
            dma((len(OFFSETS),)),
            dma((len(OFFSETS),)),
            dma((PIECES, 7)),
            dma((PIECES, 7)),
            dma((PIECES,)),
            dma((3,)),
        ],
        compiler_params=pltpu.CompilerParams(
            collective_id=0, has_side_effects=True, vmem_limit_bytes=40 << 20
        ),
        name="lamb_step",
    )(
        gradients.reshape(REPLICAS, flat),
        master.reshape(tall),
        moment.reshape(tall),
        second.reshape(tall),
        segment_ids.reshape(CHUNKS, CHUNK),
    )
    return (weights, new_master.reshape(-1), new_moment.reshape(-1), new_second.reshape(-1))


def solution(mesh):
    torus = Mesh(mesh.devices.reshape(2, 4, 4, 2, 2), AXES)
    return jax.shard_map(
        on_device,
        mesh=torus,
        in_specs=(P(DP, None, SHARD), P(DP_SHARD), P(DP_SHARD), P(DP_SHARD), P(DP_SHARD)),
        out_specs=(P(None, SHARD), P(DP_SHARD), P(DP_SHARD), P(DP_SHARD)),
        check_vma=False,
    )
```

time: 133 us -> 68.4 us (0.51)
  blocking collectives: 90.7 us -> 0 us
  Pallas kernels: 0 us -> 58.3 us
  other arithmetic: 20.4 us -> 0 us
  local copies, waits for them, and re-layouts: 18.7 us -> 8.53 us
    pallas_call x0 -> x1, Pallas kernels: none -> 58.3 us  [on_device(): pl.pallas_call(kernel, out_shape=(jax.ShapeDtypeStruct((REPLICAS, flat),...]
    all_to_all x2 -> x0, blocking collectives: 57 us -> none  [the longest x1 30.4 us: on_device(): lax.all_to_all(gradients[0], DP, split_axis=0, concat_axis=0, tiled=True)]
    psum x5 -> x0, blocking collectives: 33.7 us -> none  [one_axis_at_a_time(): array = lax.psum(array, axis)]
    broadcast_in_dim x1 -> x0, other arithmetic: 11.6 us -> none  [copy_for_each(): copies = jnp.broadcast_to(array, (lax.axis_size(axis), *array.shape))]
    unnamed x17 -> x14, local copies, waits for them, and re-layouts: 16.6 us -> 8.53 us
    reduce_sum x2 -> x0, other arithmetic: 4.59 us -> none  [the longest x1 4.14 us: on_device(): summed = jnp.sum(received.astype(jnp.float32), axis=0)]
    all_to_all x1 -> x0, other arithmetic: 3.23 us -> none  [on_device(): lax.all_to_all(gradients[0], DP, split_axis=0, concat_axis=0, tiled=True)]
    broadcast_in_dim x1 -> x0, local copies, waits for them, and re-layouts: 1.62 us -> none  [copy_for_each(): copies = jnp.broadcast_to(array, (lax.axis_size(axis), *array.shape))]
where the time goes in v1:
time: 68.4 us; the launch traced here: 67.5 us
  Pallas kernels  58.3 us (85%)
  local copies, waits for them, and re-layouts  8.53 us (12%)
    pallas_call x1, Pallas kernels, on_device(): pl.pallas_call(kernel, out_shape=(jax.ShapeDtypeStruct((REPLICAS, flat),...  58.3 us
    unnamed x14, local copies, waits for them, and re-layouts  8.53 us

profile of v1, /device:TPU:0, one launch (start us, length us, event | category | flops | bytes accessed | tf_op | source)
XLA Modules:
  0.0 67.5 jit_solution(1778588294657978786)
XLA Ops:
  0.6 0.0 copy-start
  0.6 1.4 %copy-done = bf16[1,8,98304]{2,1,0:T(8,128)(2,1)S(1)} copy-done((bf16[1,8,98304]{2,1,0:T(8,128)(2,1)S(1)}, bf16[1,8,98304]{2,1,0:T(8,128)(2,1)}, u32[]{:S(2)}) %copy-start) | copy-done | bytes 1572888
  2.0 0.0 copy-start.1
  2.0 1.0 %copy-done.1 = f32[98304]{0:T(1024)S(1)} copy-done((f32[98304]{0:T(1024)S(1)}, f32[98304]{0:T(1024)}, u32[]{:S(2)}) %copy-start.1) | copy-done | bytes 393240
  3.0 0.0 copy-start.2
  3.0 1.0 %copy-done.2 = f32[98304]{0:T(1024)S(1)} copy-done((f32[98304]{0:T(1024)S(1)}, f32[98304]{0:T(1024)}, u32[]{:S(2)}) %copy-start.2) | copy-done | bytes 393240
  4.0 0.0 copy-start.3
  4.0 1.0 %copy-done.3 = f32[98304]{0:T(1024)S(1)} copy-done((f32[98304]{0:T(1024)S(1)}, f32[98304]{0:T(1024)}, u32[]{:S(2)}) %copy-start.3) | copy-done | bytes 393240
  5.0 0.0 copy-start.4
  5.0 0.7 %copy-done.4 = s32[768]{0:T(1024)S(1)} copy-done((s32[768]{0:T(1024)S(1)}, s32[768]{0:T(1024)}, u32[]{:S(2)}) %copy-start.4) | copy-done | bytes 3096
  5.7 58.3 %lamb_step.1 = (bf16[8,98304]{1,0:T(8,128)(2,1)S(1)}, f32[768,128]{1,0:T(8,128)S(1)}, f32[768,128]{1,0:T(8,128)S(1)}, f32[768,128]{1,0:T(8,128)S(1)}) custom-call(bf16[8,98304]{1,0:T(8,128)(2,1)S(1)} %bitcast.8, f32[768,128]{1,0:T(8,128)S(1)} %bitcast.12, f32[768,128]{1,0:T(8,128)S(1)} %bitcast.13, f32[768,128]{1,0:T(8,128)S(1)} %bitcast.14, ...), custom_call_target="tpu_custom_call" | custom-call | tf_op jit(solution)/shard_map/lamb_step/pallas_call | solution.py:358
  64.0 1.1 %copy.13 = bf16[8,98304]{1,0:T(8,128)(2,1)} copy(bf16[8,98304]{1,0:T(8,128)(2,1)S(1)} %get-tuple-element.16) | data formatting | bytes 3145728
  65.1 0.8 %copy.14 = f32[98304]{0:T(1024)} copy(f32[98304]{0:T(1024)S(1)} %bitcast.11) | data formatting | bytes 786432
  65.9 0.8 %copy.15 = f32[98304]{0:T(1024)} copy(f32[98304]{0:T(1024)S(1)} %bitcast.10) | data formatting | bytes 786432
  66.7 0.8 %copy.16 = f32[98304]{0:T(1024)} copy(f32[98304]{0:T(1024)S(1)} %bitcast.9) | data formatting | bytes 786432
Async XLA Ops:
  0.6 1.4 %copy-start = (bf16[1,8,98304]{2,1,0:T(8,128)(2,1)S(1)}, bf16[1,8,98304]{2,1,0:T(8,128)(2,1)}, u32[]{:S(2)}) copy-start(bf16[1,8,98304]{2,1,0:T(8,128)(2,1)} %param.5) | copy-start | bytes 4718596
  2.0 1.0 %copy-start.1 = (f32[98304]{0:T(1024)S(1)}, f32[98304]{0:T(1024)}, u32[]{:S(2)}) copy-start(f32[98304]{0:T(1024)} %param.6) | copy-start | bytes 1179652
  3.0 1.0 %copy-start.2 = (f32[98304]{0:T(1024)S(1)}, f32[98304]{0:T(1024)}, u32[]{:S(2)}) copy-start(f32[98304]{0:T(1024)} %param.7) | copy-start | bytes 1179652
  4.0 1.0 %copy-start.3 = (f32[98304]{0:T(1024)S(1)}, f32[98304]{0:T(1024)}, u32[]{:S(2)}) copy-start(f32[98304]{0:T(1024)} %param.8) | copy-start | bytes 1179652
  5.0 0.7 %copy-start.4 = (s32[768]{0:T(1024)S(1)}, s32[768]{0:T(1024)}, u32[]{:S(2)}) copy-start(s32[768]{0:T(1024)} %param.9) | copy-start | bytes 9220

commit v2 on v1

--- a/solution.py
+++ b/solution.py
@@ -30,10 +30,11 @@
 PIECE = 64
 PIECES = BLOCKS // PIECE
 REACH = 4
-LAG = 4
+Z_FIRST = (0, 2, 4, 6, 8, 10)
+X_FIRST = tuple(p for p in range(PIECES) if p not in Z_FIRST)
 HIGH = lax.Precision.HIGHEST
 
-STEPS = ((1, 0), (3, 0), (0, 1), (2, 1), (2, 0), (1, 1), (3, 1))
+STEPS = ((1, 1), (3, 0), (2, 1), (1, 0), (0, 1), (3, 1), (2, 0))
 X_STEPS = (1, 3, 2)
 OFFSETS = tuple(range(-REACH, 0)) + tuple(range(1, REACH + 1))
 
@@ -78,11 +79,11 @@
 
 def kernel(
     grad_hbm, master_hbm, moment_hbm, second_hbm, ids_hbm,
-    weights_out, master_out, moment_out, second_out,
-    grad_in, rows, got, master, moment, second, update, ids, squares, sums,
-    mine, theirs, spread, gathered, packed,
+    packed, master, moment, second,
+    grad_in, rows, got, update, ids, squares, sums,
+    mine, theirs, spread, gathered,
     load_sem, state_sem, send_sem, recv_sem, sum_send, sum_recv,
-    out_send, out_recv, store_sem, state_out_sem,
+    out_send, out_recv,
 ):
     here = place()
     me = row_of(here)
@@ -203,12 +204,6 @@
     ]
     for copy in swaps:
         copy.start()
-    state_stores = [
-        pltpu.make_async_copy(moment, moment_out, state_out_sem.at[0]),
-        pltpu.make_async_copy(second, second_out, state_out_sem.at[1]),
-    ]
-    for copy in state_stores:
-        copy.start()
     for copy in swaps:
         copy.wait_recv()
     total = mine[...]
@@ -248,54 +243,32 @@
         block = gathered.at[row_of(behind[j]), piece_of(p)]
         return remote(block, block, out_send.at[p, 4 + j], out_recv.at[p, 4 + j], partner)
 
-    def finish_chunk(c, carry):
+    def finish_chunk(c):
         trust_block = lax.dot_general(
             onehot(c), trust_of, (((0,), (0,)), ((), ())), precision=HIGH,
             preferred_element_type=jnp.float32,
         )
-        part = pl.ds(pl.multiple_of(c * CHUNK, CHUNK), CHUNK)
+        part = pl.ds(c * CHUNK, CHUNK)
         new_master = master[part, :] - learn_rate * (update[part, :] * trust_block)
         master[part, :] = new_master
         gathered[me, part, :] = new_master.astype(jnp.bfloat16)
-        for half in range(CHUNK // PIECE):
-            for i in range(4):
-                direct(c * (CHUNK // PIECE) + half, i).start()
-        return carry
-
-    lax.fori_loop(0, CHUNKS, finish_chunk, 0)
-    state_stores.append(pltpu.make_async_copy(master, master_out, state_out_sem.at[2]))
-    state_stores[2].start()
-
-    def z_first(p):
-        return lax.rem(p * 5, 12) < 5
-
-    def forward(p):
-        @pl.when(z_first(p))
-        def _():
-            arrived(p, 0, partner).wait_recv()
-            for j in range(3):
-                onward_x(p, j).start()
-
-        @pl.when(jnp.logical_not(z_first(p)))
-        def _():
+
+    def forward_x(p):
+        arrived(p, 0, partner).wait_recv()
+        for j in range(3):
+            onward_x(p, j).start()
+
+    def forward_z(p):
+        for j in range(3):
+            arrived(p, 1 + j, behind[j]).wait_recv()
+            onward_z(p, j).start()
+
+    def collect(p):
+        if p in Z_FIRST:
             for j in range(3):
                 arrived(p, 1 + j, behind[j]).wait_recv()
-                onward_z(p, j).start()
-
-    def store(p):
-        cols = pl.ds(pl.multiple_of(p * PIECE * LANES, PIECE * LANES), PIECE * LANES)
-        return pltpu.make_async_copy(packed.at[:, cols], weights_out.at[:, cols], store_sem.at[p])
-
-    def collect(p):
-        @pl.when(z_first(p))
-        def _():
-            for j in range(3):
-                arrived(p, 1 + j, behind[j]).wait_recv()
-
-        @pl.when(jnp.logical_not(z_first(p)))
-        def _():
+        else:
             arrived(p, 0, partner).wait_recv()
-
         for j in range(3):
             arrived(p, 4 + j, far_from[j]).wait_recv()
         for r in range(REPLICAS):
@@ -311,20 +284,27 @@
             return carry
 
         lax.fori_loop(0, PIECE // 8, tile, 0)
-        store(p).start()
-
-    def gather_step(s, carry):
-        @pl.when(s < PIECES)
-        def _():
-            forward(s)
-
-        @pl.when(s >= LAG)
-        def _():
-            collect(s - LAG)
-
-        return carry
-
-    lax.fori_loop(0, PIECES + LAG, gather_step, 0)
+
+    for c in range(CHUNKS):
+        finish_chunk(c)
+        for p in range(c * PIECES // CHUNKS, (c + 1) * PIECES // CHUNKS):
+            if p in Z_FIRST:
+                direct(p, 0).start()
+            else:
+                for i in range(1, 4):
+                    direct(p, i).start()
+    for p in X_FIRST:
+        direct(p, 0).start()
+    for k in range(max(len(Z_FIRST), len(X_FIRST))):
+        if k < len(Z_FIRST):
+            for i in range(1, 4):
+                direct(Z_FIRST[k], i).start()
+        if k < len(X_FIRST):
+            forward_z(X_FIRST[k])
+        if k < len(Z_FIRST):
+            forward_x(Z_FIRST[k])
+    for p in X_FIRST + Z_FIRST:
+        collect(p)
 
     def drain(c, carry):
         for k in range(len(STEPS)):
@@ -339,13 +319,19 @@
                 gathered.at[me, piece_of(p)], gathered.at[me, piece_of(p)],
                 out_send.at[p, i], out_recv.at[p, i], partner,
             ).wait_send()
-        store(p).wait()
         return carry
 
     lax.fori_loop(0, PIECES, drain_out, 0)
     for copy in swaps:
         copy.wait_send()
-    for copy in state_stores:
+
+
+def hand_over(*refs):
+    sem = refs[-1]
+    copies = [pltpu.make_async_copy(refs[i], refs[4 + i], sem.at[i]) for i in range(4)]
+    for copy in copies:
+        copy.start()
+    for copy in copies:
         copy.wait()
 
 
@@ -353,7 +339,7 @@
     flat = master.shape[0]
     tall = (BLOCKS, LANES)
     f32, bf16 = jnp.float32, jnp.bfloat16
-    any_spec = pl.BlockSpec(memory_space=pl.ANY)
+    vmem_spec = pl.BlockSpec(memory_space=pltpu.VMEM)
     dma = pltpu.SemaphoreType.DMA
     weights, new_master, new_moment, new_second = pl.pallas_call(
         kernel,
@@ -364,14 +350,11 @@
             jax.ShapeDtypeStruct(tall, f32),
         ),
         in_specs=[pl.BlockSpec(memory_space=pltpu.HBM)] * 5,
-        out_specs=(any_spec,) * 4,
+        out_specs=(vmem_spec,) * 4,
         scratch_shapes=[
             pltpu.VMEM((REPLICAS, flat), bf16),
             pltpu.VMEM((REPLICAS, BLOCKS, LANES), bf16),
             pltpu.VMEM((len(STEPS), BLOCKS, LANES), bf16),
-            pltpu.VMEM(tall, f32),
-            pltpu.VMEM(tall, f32),
-            pltpu.VMEM(tall, f32),
             pltpu.VMEM(tall, f32),
             pltpu.VMEM((CHUNKS, CHUNK), jnp.int32),
             pltpu.VMEM((CHUNK, LANES), f32),
@@ -380,7 +363,6 @@
             pltpu.VMEM((len(OFFSETS), 8, LANES), f32),
             pltpu.VMEM((CHUNK * 8, LANES), f32),
             pltpu.VMEM((REPLICAS, BLOCKS, LANES), bf16),
-            pltpu.VMEM((REPLICAS, flat), bf16),
             dma((CHUNKS,)),
             dma((4,)),
             dma((CHUNKS, len(STEPS))),
@@ -389,20 +371,37 @@
             dma((len(OFFSETS),)),
             dma((PIECES, 7)),
             dma((PIECES, 7)),
-            dma((PIECES,)),
-            dma((3,)),
         ],
         compiler_params=pltpu.CompilerParams(
             collective_id=0, has_side_effects=True, vmem_limit_bytes=40 << 20
         ),
         name="lamb_step",
     )(
-        gradients.reshape(REPLICAS, flat),
-        master.reshape(tall),
-        moment.reshape(tall),
-        second.reshape(tall),
-        segment_ids.reshape(CHUNKS, CHUNK),
+        *(
+            pltpu.with_memory_space_constraint(array, pltpu.HBM)
+            for array in (
+                gradients.reshape(REPLICAS, flat),
+                master.reshape(tall),
+                moment.reshape(tall),
+                second.reshape(tall),
+                segment_ids.reshape(CHUNKS, CHUNK),
+            )
+        )
     )
+    weights, new_master, new_moment, new_second = pl.pallas_call(
+        hand_over,
+        out_shape=(
+            jax.ShapeDtypeStruct((REPLICAS, flat), bf16),
+            jax.ShapeDtypeStruct(tall, f32),
+            jax.ShapeDtypeStruct(tall, f32),
+            jax.ShapeDtypeStruct(tall, f32),
+        ),
+        in_specs=[vmem_spec] * 4,
+        out_specs=(pl.BlockSpec(memory_space=pltpu.HBM),) * 4,
+        scratch_shapes=[dma((4,))],
+        compiler_params=pltpu.CompilerParams(vmem_limit_bytes=8 << 20),
+        name="hand_over",
+    )(weights, new_master, new_moment, new_second)
     return (weights, new_master.reshape(-1), new_moment.reshape(-1), new_second.reshape(-1))
 
 

time: 68.4 us -> 53.6 us (0.78)
  local copies, waits for them, and re-layouts: 8.53 us -> 0 us
  Pallas kernels: 58.3 us -> 52.3 us
    unnamed x14 -> x0, local copies, waits for them, and re-layouts: 8.53 us -> none
    pallas_call x1, Pallas kernels: 58.3 us -> 50.8 us  [on_device(): pl.pallas_call(kernel, out_shape=(jax.ShapeDtypeStruct((REPLICAS, flat),...]
    pallas_call x0 -> x1, Pallas kernels: none -> 1.56 us  [on_device(): pl.pallas_call(hand_over, out_shape=(jax.ShapeDtypeStruct((REPLICAS, flat...]
where the time goes in v2:
time: 53.6 us; the launch traced here: 53 us
  Pallas kernels  52.3 us (98%)
  between operations  0.64 us (1%)
    pallas_call x1, Pallas kernels, on_device(): pl.pallas_call(kernel, out_shape=(jax.ShapeDtypeStruct((REPLICAS, flat),...  50.8 us
    pallas_call x1, Pallas kernels, on_device(): pl.pallas_call(hand_over, out_shape=(jax.ShapeDtypeStruct((REPLICAS, flat...  1.56 us

profile of v2, /device:TPU:0, one launch (start us, length us, event | category | flops | bytes accessed | tf_op | source)
XLA Modules:
  0.0 53.0 jit_solution(5228880119986641238)
XLA Ops:
  0.6 50.8 %lamb_step.1 = (bf16[8,98304]{1,0:T(8,128)(2,1)S(1)}, f32[768,128]{1,0:T(8,128)S(1)}, f32[768,128]{1,0:T(8,128)S(1)}, f32[768,128]{1,0:T(8,128)S(1)}) custom-call(bf16[8,98304]{1,0:T(8,128)(2,1)} %bitcast.8, f32[768,128]{1,0:T(8,128)} %bitcast.9, f32[768,128]{1,0:T(8,128)} %bitcast.10, f32[768,128]{1,0:T(8,128)} %bitcast.11, s32[6,128]{1,0:T(8,128)} %bitcast.12), custom_call_target="tpu_custom_call" | custom-call | tf_op jit(solution)/shard_map/lamb_step/pallas_call | solution.py:344
  51.4 1.6 %hand_over.1 = (bf16[8,98304]{1,0:T(8,128)(2,1)}, f32[768,128]{1,0:T(8,128)}, f32[768,128]{1,0:T(8,128)}, f32[768,128]{1,0:T(8,128)}) custom-call(bf16[8,98304]{1,0:T(8,128)(2,1)S(1)} %get-tuple-element.12.refs_0_, f32[768,128]{1,0:T(8,128)S(1)} %get-tuple-element.13.refs_1_, f32[768,128]{1,0:T(8,128)S(1)} %get-tuple-element.14.refs_2_, ...), custom_call_target="tpu_custom_call" | custom-call | tf_op jit(solution)/shard_map/hand_over/pallas_call | solution.py:391

commit v3 on v2

--- a/solution.py
+++ b/solution.py
@@ -90,6 +90,10 @@
     peers = [replica_at(here, a, b) for a, b in STEPS]
     neighbours = [flat_neighbour(here, k) for k in OFFSETS]
 
+    barrier = pltpu.get_barrier_semaphore()
+    for there in peers + neighbours:
+        pl.semaphore_signal(barrier, inc=1, device_id=there, device_id_type=MESH)
+
     def load(c):
         cols = pl.ds(pl.multiple_of(c * CHUNK * LANES, CHUNK * LANES), CHUNK * LANES)
         return pltpu.make_async_copy(grad_hbm.at[:, cols], grad_in.at[:, cols], load_sem.at[c])
@@ -104,10 +108,6 @@
     ]
     for copy in state_loads:
         copy.start()
-
-    barrier = pltpu.get_barrier_semaphore()
-    for there in peers + neighbours:
-        pl.semaphore_signal(barrier, inc=1, device_id=there, device_id_type=MESH)
 
     def split_rows(c):
         load(c).wait()
@@ -133,8 +133,12 @@
         part = pl.ds(pl.multiple_of(c * CHUNK, CHUNK), CHUNK)
         return remote(
             rows.at[row_of(peers[k]), part], got.at[k, part],
-            send_sem.at[c, k], recv_sem.at[c, k], peers[k],
-        )
+            send_sem, recv_sem.at[c], peers[k],
+        )
+
+    def await_chunk(c):
+        part = got.at[:, pl.ds(pl.multiple_of(c * CHUNK, CHUNK), CHUNK)]
+        remote(part, part, send_sem, recv_sem.at[c], peers[0]).wait_recv()
 
     def send_chunk(c, carry):
         split_rows(c)
@@ -168,8 +172,7 @@
     lax.fori_loop(0, CHUNKS, weigh, 0)
 
     def step_chunk(c, carry):
-        for k in range(len(STEPS)):
-            exchange(c, k).wait_recv()
+        await_chunk(c)
         for h in range(CHUNK // SUB):
             part = pl.ds(pl.multiple_of(c * CHUNK + h * SUB, SUB), SUB)
             total = rows[me, part, :].astype(jnp.float32)
@@ -199,13 +202,13 @@
         preferred_element_type=jnp.float32,
     )
     swaps = [
-        remote(mine, theirs.at[i], sum_send.at[i], sum_recv.at[i], neighbours[len(OFFSETS) - 1 - i])
+        remote(mine, theirs.at[i], sum_send, sum_recv, neighbours[len(OFFSETS) - 1 - i])
         for i in range(len(OFFSETS))
     ]
     for copy in swaps:
         copy.start()
-    for copy in swaps:
-        copy.wait_recv()
+    all_swaps = remote(theirs, theirs, sum_send, sum_recv, neighbours[0])
+    all_swaps.wait_recv()
     total = mine[...]
     for i in range(len(OFFSETS)):
         total = total + theirs[i]
@@ -221,27 +224,29 @@
     beside = [replica_at(here, a, 0) for a in X_STEPS]
     behind = [replica_at(here, 4 - a, 0) for a in X_STEPS]
     direct_to = [partner] + beside
-    direct_from = [partner] + behind
-    far_from = [replica_at(here, 4 - a, 1) for a in X_STEPS]
 
     def piece_of(p):
         return pl.ds(pl.multiple_of(p * PIECE, PIECE), PIECE)
 
     def direct(p, i):
         block = gathered.at[me, piece_of(p)]
-        return remote(block, block, out_send.at[p, i], out_recv.at[p, i], direct_to[i])
-
-    def arrived(p, i, source):
-        block = gathered.at[row_of(source), piece_of(p)]
-        return remote(block, block, out_send.at[p, i], out_recv.at[p, i], partner)
+        if p in Z_FIRST:
+            sem = 0 if i == 0 else 1
+        else:
+            sem = (2, 0, 0, 1)[i]
+        return remote(block, block, out_send, out_recv.at[3 * p + sem], direct_to[i])
 
     def onward_x(p, j):
         block = gathered.at[row_of(partner), piece_of(p)]
-        return remote(block, block, out_send.at[p, 4 + j], out_recv.at[p, 4 + j], beside[j])
+        return remote(block, block, out_send, out_recv.at[3 * p + 1], beside[j])
 
     def onward_z(p, j):
         block = gathered.at[row_of(behind[j]), piece_of(p)]
-        return remote(block, block, out_send.at[p, 4 + j], out_recv.at[p, 4 + j], partner)
+        return remote(block, block, out_send, out_recv.at[3 * p + 2], partner)
+
+    def await_pieces(p, sem, count):
+        blocks = got.at[pl.ds(0, count), piece_of(p)]
+        remote(blocks, blocks, out_send, out_recv.at[3 * p + sem], partner).wait_recv()
 
     def finish_chunk(c):
         trust_block = lax.dot_general(
@@ -254,23 +259,22 @@
         gathered[me, part, :] = new_master.astype(jnp.bfloat16)
 
     def forward_x(p):
-        arrived(p, 0, partner).wait_recv()
+        await_pieces(p, 0, 1)
         for j in range(3):
             onward_x(p, j).start()
 
     def forward_z(p):
-        for j in range(3):
-            arrived(p, 1 + j, behind[j]).wait_recv()
-            onward_z(p, j).start()
+        await_pieces(p, 0, 2)
+        onward_z(p, 0).start()
+        onward_z(p, 1).start()
+        await_pieces(p, 1, 1)
+        onward_z(p, 2).start()
 
     def collect(p):
         if p in Z_FIRST:
-            for j in range(3):
-                arrived(p, 1 + j, behind[j]).wait_recv()
+            await_pieces(p, 1, 6)
         else:
-            arrived(p, 0, partner).wait_recv()
-        for j in range(3):
-            arrived(p, 4 + j, far_from[j]).wait_recv()
+            await_pieces(p, 2, 4)
         for r in range(REPLICAS):
             spread[pl.ds(r, PIECE, stride=8), :] = gathered[r, piece_of(p), :].astype(jnp.float32)
 
@@ -306,24 +310,9 @@
     for p in X_FIRST + Z_FIRST:
         collect(p)
 
-    def drain(c, carry):
-        for k in range(len(STEPS)):
-            exchange(c, k).wait_send()
-        return carry
-
-    lax.fori_loop(0, CHUNKS, drain, 0)
-
-    def drain_out(p, carry):
-        for i in range(7):
-            remote(
-                gathered.at[me, piece_of(p)], gathered.at[me, piece_of(p)],
-                out_send.at[p, i], out_recv.at[p, i], partner,
-            ).wait_send()
-        return carry
-
-    lax.fori_loop(0, PIECES, drain_out, 0)
-    for copy in swaps:
-        copy.wait_send()
+    remote(got, got, send_sem, recv_sem.at[0], partner).wait_send()
+    remote(theirs, theirs, sum_send, sum_recv, partner).wait_send()
+    remote(got, got, out_send, out_recv.at[0], partner).wait_send()
 
 
 def hand_over(*refs):
@@ -365,12 +354,12 @@
             pltpu.VMEM((REPLICAS, BLOCKS, LANES), bf16),
             dma((CHUNKS,)),
             dma((4,)),
-            dma((CHUNKS, len(STEPS))),
-            dma((CHUNKS, len(STEPS))),
-            dma((len(OFFSETS),)),
-            dma((len(OFFSETS),)),
-            dma((PIECES, 7)),
-            dma((PIECES, 7)),
+            dma,
+            dma((CHUNKS,)),
+            dma,
+            dma,
+            dma,
+            dma((PIECES * 3,)),
         ],
         compiler_params=pltpu.CompilerParams(
             collective_id=0, has_side_effects=True, vmem_limit_bytes=40 << 20

time: 53.6 us -> 51.3 us (0.957)
  Pallas kernels: 52.3 us -> 50 us
    pallas_call x1, Pallas kernels: 50.8 us -> 48.5 us  [on_device(): pl.pallas_call(kernel, out_shape=(jax.ShapeDtypeStruct((REPLICAS, flat),...]
where the time goes in v3:
time: 51.3 us; the launch traced here: 50.7 us
  Pallas kernels  50 us (97%)
  between operations  0.64 us (1%)
    pallas_call x1, Pallas kernels, on_device(): pl.pallas_call(kernel, out_shape=(jax.ShapeDtypeStruct((REPLICAS, flat),...  48.5 us
    pallas_call x1, Pallas kernels, on_device(): pl.pallas_call(hand_over, out_shape=(jax.ShapeDtypeStruct((REPLICAS, flat...  1.56 us

profile of v3, /device:TPU:0, one launch (start us, length us, event | category | flops | bytes accessed | tf_op | source)
XLA Modules:
  0.0 50.7 jit_solution(112538318352976851)
XLA Ops:
  0.6 48.5 %lamb_step.1 = (bf16[8,98304]{1,0:T(8,128)(2,1)S(1)}, f32[768,128]{1,0:T(8,128)S(1)}, f32[768,128]{1,0:T(8,128)S(1)}, f32[768,128]{1,0:T(8,128)S(1)}) custom-call(bf16[8,98304]{1,0:T(8,128)(2,1)} %bitcast.8, f32[768,128]{1,0:T(8,128)} %bitcast.9, f32[768,128]{1,0:T(8,128)} %bitcast.10, f32[768,128]{1,0:T(8,128)} %bitcast.11, s32[6,128]{1,0:T(8,128)} %bitcast.12), custom_call_target="tpu_custom_call" | custom-call | tf_op jit(solution)/shard_map/lamb_step/pallas_call | solution.py:333
  49.1 1.6 %hand_over.1 = (bf16[8,98304]{1,0:T(8,128)(2,1)}, f32[768,128]{1,0:T(8,128)}, f32[768,128]{1,0:T(8,128)}, f32[768,128]{1,0:T(8,128)}) custom-call(bf16[8,98304]{1,0:T(8,128)(2,1)S(1)} %get-tuple-element.12.refs_0_, f32[768,128]{1,0:T(8,128)S(1)} %get-tuple-element.13.refs_1_, f32[768,128]{1,0:T(8,128)S(1)} %get-tuple-element.14.refs_2_, ...), custom_call_target="tpu_custom_call" | custom-call | tf_op jit(solution)/shard_map/hand_over/pallas_call | solution.py:380

commit v4 on v3

--- a/solution.py
+++ b/solution.py
@@ -32,10 +32,13 @@
 REACH = 4
 Z_FIRST = (0, 2, 4, 6, 8, 10)
 X_FIRST = tuple(p for p in range(PIECES) if p not in Z_FIRST)
+LAG = 3
 HIGH = lax.Precision.HIGHEST
 
 STEPS = ((1, 1), (3, 0), (2, 1), (1, 0), (0, 1), (3, 1), (2, 0))
 X_STEPS = (1, 3, 2)
+ROUTES = ("plane", "plane", 1, 3, "direct", "direct")
+SUMMED = tuple(c for c in range(CHUNKS) if ROUTES[c] != "direct")
 OFFSETS = tuple(range(-REACH, 0)) + tuple(range(1, REACH + 1))
 
 
@@ -80,7 +83,7 @@
 def kernel(
     grad_hbm, master_hbm, moment_hbm, second_hbm, ids_hbm,
     packed, master, moment, second,
-    grad_in, rows, got, update, ids, squares, sums,
+    grad_in, rows, got, sum_out, sum_in, update, ids, picks, squares, sums,
     mine, theirs, spread, gathered,
     load_sem, state_sem, send_sem, recv_sem, sum_send, sum_recv,
     out_send, out_recv,
@@ -129,29 +132,72 @@
                     jnp.bfloat16
                 )
 
-    def exchange(c, k):
-        part = pl.ds(pl.multiple_of(c * CHUNK, CHUNK), CHUNK)
-        return remote(
-            rows.at[row_of(peers[k]), part], got.at[k, part],
-            send_sem, recv_sem.at[c], peers[k],
-        )
-
-    def await_chunk(c):
-        part = got.at[:, pl.ds(pl.multiple_of(c * CHUNK, CHUNK), CHUNK)]
-        remote(part, part, send_sem, recv_sem.at[c], peers[0]).wait_recv()
-
-    def send_chunk(c, carry):
+    def part_of(c):
+        return pl.ds(c * CHUNK, CHUNK)
+
+    partner = replica_at(here, 0, 1)
+
+    def sends(c):
+        route = ROUTES[c]
+        if route == "direct":
+            return [(there, there, k) for k, there in enumerate(peers)]
+        if route == "plane":
+            out = []
+            for j, a in enumerate(X_STEPS):
+                there = replica_at(here, a, 0)
+                out.append((replica_at(here, a, 1), there, 3 + j))
+                out.append((there, there, j))
+            return out
+        near, back = route, 4 - route
+        return [
+            (replica_at(here, 2, 1), replica_at(here, back, 1), 4),
+            (replica_at(here, 2, 0), replica_at(here, back, 0), 3),
+            (replica_at(here, back, 1), partner, 5),
+            (replica_at(here, near, 1), replica_at(here, near, 1), 1),
+            (partner, partner, 2),
+            (replica_at(here, near, 0), replica_at(here, near, 0), 0),
+        ]
+
+    def sum_target(c):
+        return partner if ROUTES[c] == "plane" else replica_at(here, 4 - ROUTES[c], 0)
+
+    def send_rows(c):
+        for owner, there, slot in sends(c):
+            direct_route = ROUTES[c] == "direct"
+            remote(
+                rows.at[row_of(owner), part_of(c)], got.at[slot, part_of(c)],
+                send_sem.at[1 if direct_route else 0],
+                recv_sem.at[c, 1 if slot >= 3 and not direct_route else 0], there,
+            ).start()
+
+    def await_rows(c, stage, first, count):
+        part = got.at[pl.ds(first, count), part_of(c)]
+        remote(part, part, send_sem.at[0], recv_sem.at[c, stage], partner).wait_recv()
+
+    def send_sum(c):
+        await_rows(c, 1, 3, 3)
+        there = sum_target(c)
+        owner = row_of(there)
+
+        def add(h, carry):
+            part = pl.ds(pl.multiple_of(c * CHUNK + h * SUB, SUB), SUB)
+            total = rows[owner, part, :].astype(jnp.float32)
+            for k in range(3, 6):
+                total = total + got[k, part, :].astype(jnp.float32)
+            sum_out[part, :] = total
+            return carry
+
+        lax.fori_loop(0, CHUNK // SUB, add, 0)
+        remote(
+            sum_out.at[part_of(c)], sum_in.at[part_of(c)],
+            send_sem.at[0], recv_sem.at[c, 0], there,
+        ).start()
+
+    for c in range(CHUNKS):
         split_rows(c)
-
-        @pl.when(c == 0)
-        def _():
+        if c == 0:
             pl.semaphore_wait(barrier, len(peers) + len(neighbours))
-
-        for k in range(len(STEPS)):
-            exchange(c, k).start()
-        return carry
-
-    lax.fori_loop(0, CHUNKS, send_chunk, 0)
+        send_rows(c)
 
     for copy in state_loads:
         copy.wait()
@@ -161,6 +207,17 @@
         return (tensor == ids[pl.ds(c, 1), :]).astype(jnp.float32)
 
     sums[...] = jnp.zeros_like(sums)
+    wide = lax.broadcasted_iota(jnp.int32, (2 * TENSORS, LANES), 0)
+    lane = lax.broadcasted_iota(jnp.int32, (2 * TENSORS, LANES), 1)
+    upper = wide < TENSORS
+    tensor_of = jnp.where(upper, wide, wide - TENSORS)
+
+    def index_blocks(c, carry):
+        chosen = (tensor_of == ids[pl.ds(c, 1), :]).astype(jnp.float32)
+        picks[pl.ds(pl.multiple_of(c * CHUNK, CHUNK), CHUNK), :] = chosen.T.astype(jnp.bfloat16)
+        return carry
+
+    lax.fori_loop(0, CHUNKS, index_blocks, 0)
 
     def weigh(c, carry):
         values = master[pl.ds(pl.multiple_of(c * CHUNK, CHUNK), CHUNK), :]
@@ -171,13 +228,17 @@
 
     lax.fori_loop(0, CHUNKS, weigh, 0)
 
-    def step_chunk(c, carry):
-        await_chunk(c)
-        for h in range(CHUNK // SUB):
+    def step_chunk(c):
+        direct_route = ROUTES[c] == "direct"
+        await_rows(c, 0, 0, 7 if direct_route else 5)
+
+        def step(h, carry):
             part = pl.ds(pl.multiple_of(c * CHUNK + h * SUB, SUB), SUB)
             total = rows[me, part, :].astype(jnp.float32)
-            for k in range(len(STEPS)):
+            for k in range(7 if direct_route else 3):
                 total = total + got[k, part, :].astype(jnp.float32)
+            if not direct_route:
+                total = total + sum_in[part, :]
             grad = total / REPLICAS
             next_moment = 0.9 * moment[part, :] + 0.1 * grad
             next_second = 0.999 * second[part, :] + 0.001 * grad * grad
@@ -188,18 +249,23 @@
             moment[part, :] = next_moment
             second[part, :] = next_second
             update[part, :] = change
-            squares[pl.ds(h * SUB, SUB), :] = change * change
+            squares[pl.ds(pl.multiple_of(h * SUB, SUB), SUB), :] = change * change
+            return carry
+
+        lax.fori_loop(0, CHUNK // SUB, step, 0)
         sums[TENSORS:, :] += jnp.dot(
             onehot(c), squares[...], precision=HIGH, preferred_element_type=jnp.float32
         )
-        return carry
-
-    lax.fori_loop(0, CHUNKS, step_chunk, 0)
-
-    ones = jnp.ones((8, LANES), jnp.float32)
-    mine[...] = lax.dot_general(
-        ones, sums[...], (((1,), (1,)), ((), ())), precision=HIGH,
-        preferred_element_type=jnp.float32,
+
+    for c in range(CHUNKS + LAG):
+        if c in SUMMED:
+            send_sum(c)
+        if c >= LAG:
+            step_chunk(c - LAG)
+
+    per_tensor = jnp.sum(sums[...], axis=1, keepdims=True)
+    mine[...] = jnp.broadcast_to(
+        jnp.sum(jnp.where(wide == lane, per_tensor, 0.0), axis=0, keepdims=True), (8, LANES)
     )
     swaps = [
         remote(mine, theirs.at[i], sum_send, sum_recv, neighbours[len(OFFSETS) - 1 - i])
@@ -214,13 +280,14 @@
         total = total + theirs[i]
     trust = jnp.sqrt(total) / (jnp.sqrt(pltpu.roll(total, TENSORS, 1)) + tiny_eps)
     trust_row = trust[:1, :]
-    diagonal = lax.broadcasted_iota(jnp.int32, (TENSORS, LANES), 0) == lax.broadcasted_iota(
-        jnp.int32, (TENSORS, LANES), 1
-    )
-    trust_of = jnp.sum(jnp.where(diagonal, trust_row, 0.0), axis=1, keepdims=True)
-    trust_of = jnp.broadcast_to(trust_of, (TENSORS, LANES))
-
-    partner = replica_at(here, 0, 1)
+    trust_of = jnp.sum(jnp.where(tensor_of == lane, trust_row, 0.0), axis=1, keepdims=True)
+    trust_of = jnp.broadcast_to(trust_of, (2 * TENSORS, LANES))
+    high = trust_of.astype(jnp.bfloat16).astype(jnp.float32)
+    middle = (trust_of - high).astype(jnp.bfloat16).astype(jnp.float32)
+    low = trust_of - high - middle
+    first_terms = jnp.where(upper, high, middle).astype(jnp.bfloat16)
+    last_term = jnp.where(upper, low, 0.0).astype(jnp.bfloat16)
+
     beside = [replica_at(here, a, 0) for a in X_STEPS]
     behind = [replica_at(here, 4 - a, 0) for a in X_STEPS]
     direct_to = [partner] + beside
@@ -248,12 +315,12 @@
         blocks = got.at[pl.ds(0, count), piece_of(p)]
         remote(blocks, blocks, out_send, out_recv.at[3 * p + sem], partner).wait_recv()
 
-    def finish_chunk(c):
-        trust_block = lax.dot_general(
-            onehot(c), trust_of, (((0,), (0,)), ((), ())), precision=HIGH,
-            preferred_element_type=jnp.float32,
-        )
-        part = pl.ds(c * CHUNK, CHUNK)
+    def finish_piece(p):
+        part = pl.ds(p * PIECE, PIECE)
+        pick = picks[part, :]
+        trust_block = jnp.dot(
+            pick, first_terms, preferred_element_type=jnp.float32
+        ) + jnp.dot(pick, last_term, preferred_element_type=jnp.float32)
         new_master = master[part, :] - learn_rate * (update[part, :] * trust_block)
         master[part, :] = new_master
         gathered[me, part, :] = new_master.astype(jnp.bfloat16)
@@ -289,14 +356,13 @@
 
         lax.fori_loop(0, PIECE // 8, tile, 0)
 
-    for c in range(CHUNKS):
-        finish_chunk(c)
-        for p in range(c * PIECES // CHUNKS, (c + 1) * PIECES // CHUNKS):
-            if p in Z_FIRST:
-                direct(p, 0).start()
-            else:
-                for i in range(1, 4):
-                    direct(p, i).start()
+    for p in range(PIECES):
+        finish_piece(p)
+        if p in Z_FIRST:
+            direct(p, 0).start()
+        else:
+            for i in range(1, 4):
+                direct(p, i).start()
     for p in X_FIRST:
         direct(p, 0).start()
     for k in range(max(len(Z_FIRST), len(X_FIRST))):
@@ -310,7 +376,12 @@
     for p in X_FIRST + Z_FIRST:
         collect(p)
 
-    remote(got, got, send_sem, recv_sem.at[0], partner).wait_send()
+    shared = rows.at[:, pl.ds(0, len(SUMMED) * CHUNK)]
+    remote(shared, shared, send_sem.at[0], recv_sem.at[0, 0], partner).wait_send()
+    for c in range(CHUNKS):
+        if c not in SUMMED:
+            straight = got.at[:, part_of(c)]
+            remote(straight, straight, send_sem.at[1], recv_sem.at[c, 0], partner).wait_send()
     remote(theirs, theirs, sum_send, sum_recv, partner).wait_send()
     remote(got, got, out_send, out_recv.at[0], partner).wait_send()
 
@@ -345,7 +416,10 @@
             pltpu.VMEM((REPLICAS, BLOCKS, LANES), bf16),
             pltpu.VMEM((len(STEPS), BLOCKS, LANES), bf16),
             pltpu.VMEM(tall, f32),
+            pltpu.VMEM(tall, f32),
+            pltpu.VMEM(tall, f32),
             pltpu.VMEM((CHUNKS, CHUNK), jnp.int32),
+            pltpu.VMEM((BLOCKS, LANES), bf16),
             pltpu.VMEM((CHUNK, LANES), f32),
             pltpu.VMEM((2 * TENSORS, LANES), f32),
             pltpu.VMEM((8, LANES), f32),
@@ -354,8 +428,8 @@
             pltpu.VMEM((REPLICAS, BLOCKS, LANES), bf16),
             dma((CHUNKS,)),
             dma((4,)),
-            dma,
-            dma((CHUNKS,)),
+            dma((2,)),
+            dma((CHUNKS, 2)),
             dma,
             dma,
             dma,

time: 51.3 us -> 50.3 us (0.981)
  Pallas kernels: 50 us -> 49.1 us
    pallas_call x1, Pallas kernels: 48.5 us -> 47.5 us  [on_device(): pl.pallas_call(kernel, out_shape=(jax.ShapeDtypeStruct((REPLICAS, flat),...]
where the time goes in v4:
time: 50.3 us; the launch traced here: 49.7 us
  Pallas kernels  49.1 us (98%)
  between operations  0.64 us (1%)
    pallas_call x1, Pallas kernels, on_device(): pl.pallas_call(kernel, out_shape=(jax.ShapeDtypeStruct((REPLICAS, flat),...  47.5 us
    pallas_call x1, Pallas kernels, on_device(): pl.pallas_call(hand_over, out_shape=(jax.ShapeDtypeStruct((REPLICAS, flat...  1.56 us

profile of v4, /device:TPU:0, one launch (start us, length us, event | category | flops | bytes accessed | tf_op | source)
XLA Modules:
  0.0 49.7 jit_solution(7233882730263321850)
XLA Ops:
  0.6 47.5 %lamb_step.1 = (bf16[8,98304]{1,0:T(8,128)(2,1)S(1)}, f32[768,128]{1,0:T(8,128)S(1)}, f32[768,128]{1,0:T(8,128)S(1)}, f32[768,128]{1,0:T(8,128)S(1)}) custom-call(bf16[8,98304]{1,0:T(8,128)(2,1)} %bitcast.8, f32[768,128]{1,0:T(8,128)} %bitcast.9, f32[768,128]{1,0:T(8,128)} %bitcast.10, f32[768,128]{1,0:T(8,128)} %bitcast.11, s32[6,128]{1,0:T(8,128)} %bitcast.12), custom_call_target="tpu_custom_call" | custom-call | tf_op jit(solution)/shard_map/lamb_step/pallas_call | solution.py:404
  48.1 1.6 %hand_over.1 = (bf16[8,98304]{1,0:T(8,128)(2,1)}, f32[768,128]{1,0:T(8,128)}, f32[768,128]{1,0:T(8,128)}, f32[768,128]{1,0:T(8,128)}) custom-call(bf16[8,98304]{1,0:T(8,128)(2,1)S(1)} %get-tuple-element.12.refs_0_, f32[768,128]{1,0:T(8,128)S(1)} %get-tuple-element.13.refs_1_, f32[768,128]{1,0:T(8,128)S(1)} %get-tuple-element.14.refs_2_, ...), custom_call_target="tpu_custom_call" | custom-call | tf_op jit(solution)/shard_map/hand_over/pallas_call | solution.py:454

commit v5 on v4

--- a/solution.py
+++ b/solution.py
@@ -162,17 +162,17 @@
         return partner if ROUTES[c] == "plane" else replica_at(here, 4 - ROUTES[c], 0)
 
     def send_rows(c):
-        for owner, there, slot in sends(c):
+        for owner, there, at in sends(c):
             direct_route = ROUTES[c] == "direct"
             remote(
-                rows.at[row_of(owner), part_of(c)], got.at[slot, part_of(c)],
+                rows.at[row_of(owner), part_of(c)], got.at[at, part_of(c)],
                 send_sem.at[1 if direct_route else 0],
-                recv_sem.at[c, 1 if slot >= 3 and not direct_route else 0], there,
+                recv_sem.at[CHUNKS + SUMMED.index(c) if at >= 3 and not direct_route else c], there,
             ).start()
 
     def await_rows(c, stage, first, count):
         part = got.at[pl.ds(first, count), part_of(c)]
-        remote(part, part, send_sem.at[0], recv_sem.at[c, stage], partner).wait_recv()
+        remote(part, part, send_sem.at[0], recv_sem.at[CHUNKS + SUMMED.index(c) if stage else c], partner).wait_recv()
 
     def send_sum(c):
         await_rows(c, 1, 3, 3)
@@ -190,7 +190,7 @@
         lax.fori_loop(0, CHUNK // SUB, add, 0)
         remote(
             sum_out.at[part_of(c)], sum_in.at[part_of(c)],
-            send_sem.at[0], recv_sem.at[c, 0], there,
+            send_sem.at[0], recv_sem.at[c], there,
         ).start()
 
     for c in range(CHUNKS):
@@ -268,16 +268,14 @@
         jnp.sum(jnp.where(wide == lane, per_tensor, 0.0), axis=0, keepdims=True), (8, LANES)
     )
     swaps = [
-        remote(mine, theirs.at[i], sum_send, sum_recv, neighbours[len(OFFSETS) - 1 - i])
+        remote(mine.at[pl.ds(0, 1)], theirs.at[pl.ds(i, 1)], sum_send, sum_recv, neighbours[len(OFFSETS) - 1 - i])
         for i in range(len(OFFSETS))
     ]
     for copy in swaps:
         copy.start()
     all_swaps = remote(theirs, theirs, sum_send, sum_recv, neighbours[0])
     all_swaps.wait_recv()
-    total = mine[...]
-    for i in range(len(OFFSETS)):
-        total = total + theirs[i]
+    total = mine[...] + jnp.sum(theirs[...], axis=0, keepdims=True)
     trust = jnp.sqrt(total) / (jnp.sqrt(pltpu.roll(total, TENSORS, 1)) + tiny_eps)
     trust_row = trust[:1, :]
     trust_of = jnp.sum(jnp.where(tensor_of == lane, trust_row, 0.0), axis=1, keepdims=True)
@@ -295,25 +293,30 @@
     def piece_of(p):
         return pl.ds(pl.multiple_of(p * PIECE, PIECE), PIECE)
 
+    def slot(p):
+        if p in Z_FIRST:
+            return 2 * Z_FIRST.index(p)
+        return 2 * len(Z_FIRST) + 3 * X_FIRST.index(p)
+
     def direct(p, i):
         block = gathered.at[me, piece_of(p)]
         if p in Z_FIRST:
             sem = 0 if i == 0 else 1
         else:
             sem = (2, 0, 0, 1)[i]
-        return remote(block, block, out_send, out_recv.at[3 * p + sem], direct_to[i])
+        return remote(block, block, out_send, out_recv.at[slot(p) + sem], direct_to[i])
 
     def onward_x(p, j):
         block = gathered.at[row_of(partner), piece_of(p)]
-        return remote(block, block, out_send, out_recv.at[3 * p + 1], beside[j])
+        return remote(block, block, out_send, out_recv.at[slot(p) + 1], beside[j])
 
     def onward_z(p, j):
         block = gathered.at[row_of(behind[j]), piece_of(p)]
-        return remote(block, block, out_send, out_recv.at[3 * p + 2], partner)
+        return remote(block, block, out_send, out_recv.at[slot(p) + 2], partner)
 
     def await_pieces(p, sem, count):
         blocks = got.at[pl.ds(0, count), piece_of(p)]
-        remote(blocks, blocks, out_send, out_recv.at[3 * p + sem], partner).wait_recv()
+        remote(blocks, blocks, out_send, out_recv.at[slot(p) + sem], partner).wait_recv()
 
     def finish_piece(p):
         part = pl.ds(p * PIECE, PIECE)
@@ -377,11 +380,11 @@
         collect(p)
 
     shared = rows.at[:, pl.ds(0, len(SUMMED) * CHUNK)]
-    remote(shared, shared, send_sem.at[0], recv_sem.at[0, 0], partner).wait_send()
+    remote(shared, shared, send_sem.at[0], recv_sem.at[0], partner).wait_send()
     for c in range(CHUNKS):
         if c not in SUMMED:
             straight = got.at[:, part_of(c)]
-            remote(straight, straight, send_sem.at[1], recv_sem.at[c, 0], partner).wait_send()
+            remote(straight, straight, send_sem.at[1], recv_sem.at[c], partner).wait_send()
     remote(theirs, theirs, sum_send, sum_recv, partner).wait_send()
     remote(got, got, out_send, out_recv.at[0], partner).wait_send()
 
@@ -423,17 +426,17 @@
             pltpu.VMEM((CHUNK, LANES), f32),
             pltpu.VMEM((2 * TENSORS, LANES), f32),
             pltpu.VMEM((8, LANES), f32),
-            pltpu.VMEM((len(OFFSETS), 8, LANES), f32),
+            pltpu.VMEM((len(OFFSETS), LANES), f32),
             pltpu.VMEM((CHUNK * 8, LANES), f32),
             pltpu.VMEM((REPLICAS, BLOCKS, LANES), bf16),
             dma((CHUNKS,)),
             dma((4,)),
             dma((2,)),
-            dma((CHUNKS, 2)),
+            dma((CHUNKS + len(SUMMED),)),
             dma,
             dma,
             dma,
-            dma((PIECES * 3,)),
+            dma((len(X_FIRST) * 3 + len(Z_FIRST) * 2,)),
         ],
         compiler_params=pltpu.CompilerParams(
             collective_id=0, has_side_effects=True, vmem_limit_bytes=40 << 20

time: 50.3 us -> 49.9 us (level)
  no operation moved by 1% of the time
where the time goes in v5:
time: 49.9 us; the launch traced here: 49.3 us
  Pallas kernels  48.7 us (98%)
  between operations  0.64 us (1%)
    pallas_call x1, Pallas kernels, on_device(): pl.pallas_call(kernel, out_shape=(jax.ShapeDtypeStruct((REPLICAS, flat),...  47.1 us
    pallas_call x1, Pallas kernels, on_device(): pl.pallas_call(hand_over, out_shape=(jax.ShapeDtypeStruct((REPLICAS, flat...  1.56 us

profile of v5, /device:TPU:0, one launch (start us, length us, event | category | flops | bytes accessed | tf_op | source)
XLA Modules:
  0.0 49.3 jit_solution(10545490790132162730)
XLA Ops:
  0.6 47.1 %lamb_step.1 = (bf16[8,98304]{1,0:T(8,128)(2,1)S(1)}, f32[768,128]{1,0:T(8,128)S(1)}, f32[768,128]{1,0:T(8,128)S(1)}, f32[768,128]{1,0:T(8,128)S(1)}) custom-call(bf16[8,98304]{1,0:T(8,128)(2,1)} %bitcast.8, f32[768,128]{1,0:T(8,128)} %bitcast.9, f32[768,128]{1,0:T(8,128)} %bitcast.10, f32[768,128]{1,0:T(8,128)} %bitcast.11, s32[6,128]{1,0:T(8,128)} %bitcast.12), custom_call_target="tpu_custom_call" | custom-call | tf_op jit(solution)/shard_map/lamb_step/pallas_call | solution.py:407
  47.8 1.6 %hand_over.1 = (bf16[8,98304]{1,0:T(8,128)(2,1)}, f32[768,128]{1,0:T(8,128)}, f32[768,128]{1,0:T(8,128)}, f32[768,128]{1,0:T(8,128)}) custom-call(bf16[8,98304]{1,0:T(8,128)(2,1)S(1)} %get-tuple-element.12.refs_0_, f32[768,128]{1,0:T(8,128)S(1)} %get-tuple-element.13.refs_1_, f32[768,128]{1,0:T(8,128)S(1)} %get-tuple-element.14.refs_2_, ...), custom_call_target="tpu_custom_call" | custom-call | tf_op jit(solution)/shard_map/hand_over/pallas_call | solution.py:457

commit v6 on v5

--- a/solution.py
+++ b/solution.py
@@ -27,12 +27,12 @@
 CHUNK = 128
 CHUNKS = BLOCKS // CHUNK
 SUB = 32
-PIECE = 64
+PIECE = 128
 PIECES = BLOCKS // PIECE
 REACH = 4
-Z_FIRST = (0, 2, 4, 6, 8, 10)
+Z_FIRST = (0, 2, 4)
 X_FIRST = tuple(p for p in range(PIECES) if p not in Z_FIRST)
-LAG = 3
+LAG = 4
 HIGH = lax.Precision.HIGHEST
 
 STEPS = ((1, 1), (3, 0), (2, 1), (1, 0), (0, 1), (3, 1), (2, 0))
@@ -294,21 +294,24 @@
         return pl.ds(pl.multiple_of(p * PIECE, PIECE), PIECE)
 
     def slot(p):
-        if p in Z_FIRST:
-            return 2 * Z_FIRST.index(p)
-        return 2 * len(Z_FIRST) + 3 * X_FIRST.index(p)
+        return 3 * p
 
     def direct(p, i):
         block = gathered.at[me, piece_of(p)]
         if p in Z_FIRST:
-            sem = 0 if i == 0 else 1
+            sem = (0, 1 + Z_FIRST.index(p) % 2, 2 - Z_FIRST.index(p) % 2)[i]
         else:
             sem = (2, 0, 0, 1)[i]
         return remote(block, block, out_send, out_recv.at[slot(p) + sem], direct_to[i])
 
+    def relay(p):
+        turn = Z_FIRST.index(p) % 2
+        block = gathered.at[row_of(behind[turn]), piece_of(p)]
+        return remote(block, block, out_send, out_recv.at[slot(p) + 2], beside[turn])
+
     def onward_x(p, j):
         block = gathered.at[row_of(partner), piece_of(p)]
-        return remote(block, block, out_send, out_recv.at[slot(p) + 1], beside[j])
+        return remote(block, block, out_send, out_recv.at[slot(p) + 2], beside[j])
 
     def onward_z(p, j):
         block = gathered.at[row_of(behind[j]), piece_of(p)]
@@ -342,7 +345,7 @@
 
     def collect(p):
         if p in Z_FIRST:
-            await_pieces(p, 1, 6)
+            await_pieces(p, 2, 5)
         else:
             await_pieces(p, 2, 4)
         for r in range(REPLICAS):
@@ -366,16 +369,19 @@
         else:
             for i in range(1, 4):
                 direct(p, i).start()
+    for p in Z_FIRST:
+        direct(p, 1).start()
+        direct(p, 2).start()
     for p in X_FIRST:
         direct(p, 0).start()
     for k in range(max(len(Z_FIRST), len(X_FIRST))):
-        if k < len(Z_FIRST):
-            for i in range(1, 4):
-                direct(Z_FIRST[k], i).start()
         if k < len(X_FIRST):
             forward_z(X_FIRST[k])
         if k < len(Z_FIRST):
             forward_x(Z_FIRST[k])
+    for p in Z_FIRST:
+        await_pieces(p, 1, 1)
+        relay(p).start()
     for p in X_FIRST + Z_FIRST:
         collect(p)
 
@@ -436,7 +442,7 @@
             dma,
             dma,
             dma,
-            dma((len(X_FIRST) * 3 + len(Z_FIRST) * 2,)),
+            dma((PIECES * 3,)),
         ],
         compiler_params=pltpu.CompilerParams(
             collective_id=0, has_side_effects=True, vmem_limit_bytes=40 << 20

time: 49.9 us -> 49.3 us (0.988)
  no operation moved by 1% of the time
where the time goes in v6:
time: 49.3 us; the launch traced here: 49 us
  Pallas kernels  48.4 us (98%)
  between operations  0.64 us (1%)
    pallas_call x1, Pallas kernels, on_device(): pl.pallas_call(kernel, out_shape=(jax.ShapeDtypeStruct((REPLICAS, flat),...  46.8 us
    pallas_call x1, Pallas kernels, on_device(): pl.pallas_call(hand_over, out_shape=(jax.ShapeDtypeStruct((REPLICAS, flat...  1.56 us

profile of v6, /device:TPU:0, one launch (start us, length us, event | category | flops | bytes accessed | tf_op | source)
XLA Modules:
  0.0 49.0 jit_solution(11054417498609173893)
XLA Ops:
  0.6 46.8 %lamb_step.1 = (bf16[8,98304]{1,0:T(8,128)(2,1)S(1)}, f32[768,128]{1,0:T(8,128)S(1)}, f32[768,128]{1,0:T(8,128)S(1)}, f32[768,128]{1,0:T(8,128)S(1)}) custom-call(bf16[8,98304]{1,0:T(8,128)(2,1)} %bitcast.8, f32[768,128]{1,0:T(8,128)} %bitcast.9, f32[768,128]{1,0:T(8,128)} %bitcast.10, f32[768,128]{1,0:T(8,128)} %bitcast.11, s32[6,128]{1,0:T(8,128)} %bitcast.12), custom_call_target="tpu_custom_call" | custom-call | tf_op jit(solution)/shard_map/lamb_step/pallas_call | solution.py:413
  47.5 1.6 %hand_over.1 = (bf16[8,98304]{1,0:T(8,128)(2,1)}, f32[768,128]{1,0:T(8,128)}, f32[768,128]{1,0:T(8,128)}, f32[768,128]{1,0:T(8,128)}) custom-call(bf16[8,98304]{1,0:T(8,128)(2,1)S(1)} %get-tuple-element.12.refs_0_, f32[768,128]{1,0:T(8,128)S(1)} %get-tuple-element.13.refs_1_, f32[768,128]{1,0:T(8,128)S(1)} %get-tuple-element.14.refs_2_, ...), custom_call_target="tpu_custom_call" | custom-call | tf_op jit(solution)/shard_map/hand_over/pallas_call | solution.py:463

commit v7 on v6

--- a/solution.py
+++ b/solution.py
@@ -30,7 +30,7 @@
 PIECE = 128
 PIECES = BLOCKS // PIECE
 REACH = 4
-Z_FIRST = (0, 2, 4)
+Z_FIRST = (1, 3, 5)
 X_FIRST = tuple(p for p in range(PIECES) if p not in Z_FIRST)
 LAG = 4
 HIGH = lax.Precision.HIGHEST

time: 49.3 us -> 49.3 us (level)
  no operation moved by 1% of the time
where the time goes in v7:
time: 49.3 us; the launch traced here: 49.2 us
  Pallas kernels  48.6 us (99%)
  between operations  0.64 us (1%)
    pallas_call x1, Pallas kernels, on_device(): pl.pallas_call(kernel, out_shape=(jax.ShapeDtypeStruct((REPLICAS, flat),...  47 us
    pallas_call x1, Pallas kernels, on_device(): pl.pallas_call(hand_over, out_shape=(jax.ShapeDtypeStruct((REPLICAS, flat...  1.56 us

profile of v7, /device:TPU:0, one launch (start us, length us, event | category | flops | bytes accessed | tf_op | source)
XLA Modules:
  0.0 49.2 jit_solution(6435132817388755798)
XLA Ops:
  0.6 47.0 %lamb_step.1 = (bf16[8,98304]{1,0:T(8,128)(2,1)S(1)}, f32[768,128]{1,0:T(8,128)S(1)}, f32[768,128]{1,0:T(8,128)S(1)}, f32[768,128]{1,0:T(8,128)S(1)}) custom-call(bf16[8,98304]{1,0:T(8,128)(2,1)} %bitcast.8, f32[768,128]{1,0:T(8,128)} %bitcast.9, f32[768,128]{1,0:T(8,128)} %bitcast.10, f32[768,128]{1,0:T(8,128)} %bitcast.11, s32[6,128]{1,0:T(8,128)} %bitcast.12), custom_call_target="tpu_custom_call" | custom-call | tf_op jit(solution)/shard_map/lamb_step/pallas_call | solution.py:413
  47.6 1.6 %hand_over.1 = (bf16[8,98304]{1,0:T(8,128)(2,1)}, f32[768,128]{1,0:T(8,128)}, f32[768,128]{1,0:T(8,128)}, f32[768,128]{1,0:T(8,128)}) custom-call(bf16[8,98304]{1,0:T(8,128)(2,1)S(1)} %get-tuple-element.12.refs_0_, f32[768,128]{1,0:T(8,128)S(1)} %get-tuple-element.13.refs_1_, f32[768,128]{1,0:T(8,128)S(1)} %get-tuple-element.14.refs_2_, ...), custom_call_target="tpu_custom_call" | custom-call | tf_op jit(solution)/shard_map/hand_over/pallas_call | solution.py:463
